TPU v7x, 256 devices: a whole 4x4x8 slice. The times are simulated.
256 devices in a mesh: grp: 64 (over z, y_hi, x), rep: 4 (over y_lo, core).
Axes of the slice: x: 4, y: 4 (y_hi: 2, y_lo: 2; y = y_hi * 2 + y_lo), z: 8, core: 2. Of those that a mesh axis runs over, the one named last changes fastest.
Arguments:
- embeddings: bfloat16 [65536, 1024], P(('grp', 'rep')), may hold values from -15 to 15
- scales: float32 [65536, 8], P(('grp', 'rep')), may hold values from 0.05 to 0.5
- cluster: int32 [65536], P(('grp', 'rep')), may hold values from 0 to 767, as said below
- cluster_rank: int32 [65536], P(('grp', 'rep')), may hold values from 0 to 63, as said below
Outputs:
- best_cosine: float32 [65536], P(('grp', 'rep'))
Inputs may be any that keep to these rules, and one draw needn't show every extreme that they name: cluster // 12 names the owner of a row's cluster among 64 and cluster % 12 its place there; clusters of different shards are different even with equal numbers. Among the rows of one device at most 12 have the same owner, and in every draw some owner is named by exactly 12 rows of every device of its shard. `cluster_rank`: within one cluster the ranks of its rows are 0 to its size minus 1, each once; a cluster holds at most 64 rows, and in every draw some cluster holds exactly 64.
All inputs are finite; a program needn't handle non-finite values.
Results may differ from a plain program's by a relative error of at most 0.00035.
The roundings to bfloat16 on the way count: a program that leaves them out, or rounds other values in their place, can miss the bound.
Values may be sent and summed in bfloat16 or wider, within the bound.
A program may use at most 64 MiB of HBM per device.

v0:
```python
import jax
import jax.numpy as jnp
from jax import lax
from jax.sharding import PartitionSpec as P

CMAX = 64
STEPS = 5
COV_EPS = 0.001
UNIT_EPS = 1e-06
EXACT_MODE = lax.Precision.HIGHEST


def dequantize(embeddings, scales):
    row_count, feat_dim = embeddings.shape
    num_blocks = scales.shape[1]
    grouped = (
        embeddings.astype(jnp.float32).reshape(row_count, num_blocks, feat_dim // num_blocks)
        * scales[:, :, None]
    )
    return grouped.reshape(row_count, feat_dim).astype(jnp.bfloat16)


def covariance(gram_sum, column_total, row_total):
    average = column_total / row_total
    feat_dim = gram_sum.shape[0]
    centred = (
        gram_sum / row_total
        - average[:, None] * average[None, :]
        + COV_EPS * jnp.eye(feat_dim, dtype=jnp.float32)
    )
    normed = centred / jnp.sqrt(jnp.sum(centred * centred))
    return (average, normed)


def newton_rows(normed_rows, current_rows, first_full, spread):
    whole = first_full
    for repeat in range(STEPS - 1):
        if repeat > 0 or first_full is None:
            whole = spread(current_rows)
        product = jnp.dot(normed_rows, whole, precision=EXACT_MODE)
        product = jnp.dot(product, whole, precision=EXACT_MODE)
        product = jnp.dot(product, whole, precision=EXACT_MODE)
        current_rows = 1.5 * current_rows - 0.5 * product
    return current_rows


def whiten(values, inverse_root, average):
    offset = jnp.dot(average[None, :], inverse_root.astype(jnp.float32), precision=EXACT_MODE)
    projected = jnp.dot(values, inverse_root, preferred_element_type=jnp.float32) - offset
    energy = jnp.sum(projected * projected, axis=1, keepdims=True)
    return (projected * lax.rsqrt(energy + UNIT_EPS)).astype(jnp.bfloat16)


def best_within(table, occupied, cluster_count):
    feat_dim = table.shape[1]
    tile_rows = table.reshape(cluster_count, CMAX, feat_dim)
    similar = jnp.einsum("cmd,cnd->cmn", tile_rows, tile_rows, preferred_element_type=jnp.float32)
    present = occupied.reshape(cluster_count, CMAX)
    distinct = lax.broadcasted_iota(jnp.int32, (1, CMAX, CMAX), 1) != lax.broadcasted_iota(
        jnp.int32, (1, CMAX, CMAX), 2
    )
    allowed = present[:, :, None] & present[:, None, :] & distinct
    highest = jnp.max(jnp.where(allowed, similar, -jnp.inf), axis=2)
    return jnp.maximum(highest, -1.0).reshape(cluster_count * CMAX)


def local(embeddings, scales, cluster, cluster_rank):
    row_count, feat_dim = embeddings.shape
    values = dequantize(embeddings, scales)
    row_total = row_count * lax.axis_size("grp") * lax.axis_size("rep")
    column_part = jnp.sum(values, axis=0, dtype=jnp.float32)
    gram_sum, column_total = lax.psum(
        (
            lax.dot_general(
                values, values, (((0,), (0,)), ((), ())), preferred_element_type=jnp.float32
            ),
            column_part,
        ),
        ("grp", "rep"),
    )
    average, normed = covariance(gram_sum, column_total, row_total)
    share_rows = feat_dim // lax.axis_size("rep")
    first_row = lax.axis_index("rep") * share_rows
    first_full = 1.5 * jnp.eye(feat_dim, dtype=jnp.float32) - 0.5 * normed
    final_rows = newton_rows(
        lax.dynamic_slice_in_dim(normed, first_row, share_rows, 0),
        lax.dynamic_slice_in_dim(first_full, first_row, share_rows, 0),
        first_full,
        lambda slab_rows: lax.all_gather(slab_rows, "rep", axis=0, tiled=True),
    )
    inverse_root = lax.all_gather(final_rows.astype(jnp.bfloat16), "rep", axis=0, tiled=True)
    owner_count = lax.axis_size("grp")
    slot_rows = 3 * row_count // owner_count
    cluster_count = 3 * row_count // CMAX
    cell_count = cluster_count * CMAX
    owner_of = cluster // cluster_count
    owner_hit = (owner_of[:, None] == lax.broadcasted_iota(jnp.int32, (1, owner_count), 1)).astype(
        jnp.int32
    )
    within_pair = jnp.sum((jnp.cumsum(owner_hit, axis=0) - owner_hit) * owner_hit, axis=1)
    target = owner_of * slot_rows + within_pair
    coords = jnp.stack([cluster % cluster_count, cluster_rank], axis=1).astype(jnp.float32)
    vacant = jnp.concatenate(
        [
            jnp.full((owner_count * slot_rows, 1), cluster_count, jnp.float32),
            jnp.zeros((owner_count * slot_rows, 1), jnp.float32),
        ],
        axis=1,
    )
    labels = vacant.at[target].set(coords).astype(jnp.bfloat16).reshape(owner_count, 2 * slot_rows)
    whitened = whiten(values, inverse_root, average)
    outgoing = (
        jnp.zeros((owner_count * slot_rows, feat_dim), jnp.bfloat16)
        .at[target]
        .set(whitened)
        .reshape(owner_count, slot_rows, feat_dim)
    )
    arrived, labels_in = (
        lax.all_to_all(outgoing, "grp", split_axis=0, concat_axis=0, tiled=True),
        lax.all_to_all(labels, "grp", split_axis=0, concat_axis=0, tiled=True),
    )
    units_in = arrived.reshape(owner_count * slot_rows, feat_dim)
    placed = labels_in.reshape(owner_count * slot_rows, 2).astype(jnp.int32)
    cell_index = placed[:, 0] * CMAX + placed[:, 1]
    table = (
        jnp.zeros((cell_count, feat_dim), jnp.bfloat16).at[cell_index].set(units_in, mode="drop")
    )
    occupied = jnp.zeros((cell_count,), jnp.int32).at[cell_index].set(1, mode="drop") > 0
    highest = best_within(table, occupied, cluster_count)
    answer = highest[jnp.minimum(cell_index, cell_count - 1)].reshape(owner_count, slot_rows)
    returned = lax.all_to_all(answer, "grp", split_axis=0, concat_axis=0, tiled=True)
    return returned.reshape(owner_count * slot_rows)[target]


def solution(mesh):
    placed = (
        P(("grp", "rep"), None),
        P(("grp", "rep"), None),
        P(("grp", "rep")),
        P(("grp", "rep")),
    )
    return jax.shard_map(
        local, mesh=mesh, in_specs=placed, out_specs=P(("grp", "rep")), check_vma=False
    )
```

profile of v0, /device:TPU:2, one launch (start us, length us, event | category | flops | bytes accessed | tf_op | source)
XLA Modules:
  0.0 647.7 jit_solution(15239859383687438242)
XLA Ops:
  6.5 0.8 copy.14
  7.4 0.3 mul.102
  7.7 1.4 convert_reduce_fusion
  9.1 2.7 fusion.36
  11.8 0.0 all-reduce.2.cloned.1.call-update
  11.8 0.0 all-gather.5.cloned.1.call-start
  11.9 78.8 %psum.15 = f32[1024]{0:T(1024)S(1)} all-reduce(f32[1024]{0:T(1024)S(1)} %get-tuple-element.9), channel_id=1, replica_groups=mesh['grp'=64,'rep'=4] {'grp','rep'}, use_global_device_ids=true, to_apply=%region_7.8 | all-reduce | flops 1024 | bytes 8192 | tf_op jit(solution)/shard_map/psum | solution.py:72
  90.7 195.7 %all-reduce.2.cloned.1.call-done = f32[1024,1024]{1,0:T(8,128)} async-done(((f32[1024,1024]{1,0:T(8,128)}), f32[1024,1024]{1,0:T(8,128)}) %all-reduce.2.cloned.1.call-update) | async-done | bytes 4194320 | tf_op jit(solution)/shard_map/psum | solution.py:72
  286.3 4.2 multiply_reduce_fusion
  291.2 3.6 multiply_subtract_fusion
  294.8 3.8 fusion.14
  298.6 3.8 fusion.33
  302.5 4.8 fusion.4
  307.3 0.0 all-gather.5.cloned.1.call-update
  307.3 0.0 all-gather.7.cloned.1.call-start
  307.4 47.3 %all-gather.5.cloned.1.call-done = f32[1024,1024]{1,0:T(8,128)} async-done(((f32[256,1024]{1,0:T(8,128)}), f32[1024,1024]{1,0:T(8,128)}) %all-gather.5.cloned.1.call-update) | async-done | bytes 4194320 | tf_op jit(solution)/shard_map/all_gather | solution.py:89
  354.6 6.3 fusion.12
  361.0 3.7 fusion.37
  364.7 4.8 fusion.3
  369.6 0.0 all-gather.7.cloned.1.call-update
  369.6 0.0 all-gather.9.cloned.1.call-start
  369.6 50.1 %all-gather.7.cloned.1.call-done = f32[1024,1024]{1,0:T(8,128)} async-done(((f32[256,1024]{1,0:T(8,128)}), f32[1024,1024]{1,0:T(8,128)}) %all-gather.7.cloned.1.call-update) | async-done | bytes 4194320 | tf_op jit(solution)/shard_map/all_gather | solution.py:89
  419.7 6.6 %fusion.10 = f32[256,1024]{1,0:T(8,128)S(1)} fusion(f32[1024,1024]{1,0:T(8,128)} %all-gather.7.cloned.1.call-done, f32[1024,1024]{1,0:T(8,128)} %copy-done.3, s32[]{:T(128)S(6)} %select_n.38), kind=kOutput, calls=%fused_computation.32 | convolution fusion | flops 3221225472 | bytes 6291460 | tf_op jit(solution)/shard_map/dot_general | solution.py:40
  426.3 3.7 fusion.38
  430.1 4.8 fusion.2
  434.9 0.0 all-gather.9.cloned.1.call-update
  434.9 0.0 all-gather.11.cloned.1.call-start
  434.9 50.1 %all-gather.9.cloned.1.call-done = f32[1024,1024]{1,0:T(8,128)} async-done(((f32[256,1024]{1,0:T(8,128)}), f32[1024,1024]{1,0:T(8,128)}) %all-gather.9.cloned.1.call-update) | async-done | bytes 4194320 | tf_op jit(solution)/shard_map/all_gather | solution.py:89
  485.0 6.3 fusion.8
  491.3 3.7 fusion.39
  495.1 0.0 copy-start.7
  495.1 4.6 fusion.5
  499.7 0.0 all-gather.11.cloned.1.call-update
  499.8 0.6 reduce-window.6
  500.4 0.2 slice_reduce_fusion
  500.6 0.1 copy.12
  500.8 0.1 fusion.25
  500.9 1.3 scatter_fusion
  502.2 0.8 all_to_all.20
  503.0 13.0 %all-to-all-start = ((bf16[64,1,24]{2,1,0:T(2,128)(2,1)}), bf16[64,1,24]{2,1,0:T(2,128)(2,1)S(1)}, u32[]{:S(2)}, u32[]{:S(2)}) async-start(bf16[64,1,24]{2,1,0:T(2,128)(2,1)} %all_to_all.20), calls=%async_computation | async-start | bytes 65536 | tf_op jit(solution)/shard_map/all_to_all | solution.py:120
  516.0 17.1 %all-gather.11.cloned.1.call-done = bf16[1024,1024]{1,0:T(8,128)(2,1)} async-done(((bf16[256,1024]{1,0:T(8,128)(2,1)}), bf16[1024,1024]{1,0:T(8,128)(2,1)}) %all-gather.11.cloned.1.call-update) | async-done | bytes 2097168 | tf_op jit(solution)/shard_map/all_gather | solution.py:91
  533.1 2.5 fusion.40
  535.6 2.4 multiply_reduce_fusion.1
  538.0 2.2 scatter_custom_fusion.2
  540.2 1.5 reshape.72
  541.8 12.7 %all-to-all-start.1 = ((bf16[64,12,1024]{2,1,0:T(8,128)(2,1)}), bf16[64,12,1024]{2,1,0:T(8,128)(2,1)S(1)}, u32[]{:S(2)}, u32[]{:S(2)}) async-start(bf16[64,12,1024]{2,1,0:T(8,128)(2,1)} %reshape.72), calls=%async_computation.1 | async-start | bytes 4194304 | tf_op jit(solution)/shard_map/all_to_all | solution.py:119
  554.5 0.1 convert_reduce_fusion.1
  554.6 0.2 reshape.76
  554.8 0.4 fusion.22
  555.2 3.4 scatter_custom_fusion.1
  558.6 0.1 and.34
  558.7 46.9 %all-to-all-done.1 = bf16[64,12,1024]{2,1,0:T(8,128)(2,1)S(1)} async-done(((bf16[64,12,1024]{2,1,0:T(8,128)(2,1)}), bf16[64,12,1024]{2,1,0:T(8,128)(2,1)S(1)}, u32[]{:S(2)}, u32[]{:S(2)}) %all-to-all-start.1) | async-done | bytes 1572896 | tf_op jit(solution)/shard_map/all_to_all | solution.py:119
  605.6 1.3 reshape.121
  607.0 6.8 %scatter_custom_fusion.3 = bf16[768,1024]{1,0:T(8,128)(2,1)S(1)} fusion(s32[768]{0:T(1024)S(1)} %get-tuple-element.6, bf16[768,1024]{1,0:T(8,128)(2,1)} %reshape.121, bf16[]{:T(256)} %constant.27.clone.1), kind=kCustom, calls=%fused_computation.38 | custom fusion | bytes 1573376 | tf_op jit(solution)/shard_map/scatter | solution.py:126
  613.8 0.6 fusion.6
  614.4 0.1 max.12
  614.4 3.2 gather_fusion
  617.6 0.7 all_to_all.18
  618.3 8.4 %all-to-all-start.2 = ((f32[64,1,12]{2,1,0:T(1,128)}), f32[64,1,12]{2,1,0:T(1,128)S(1)}, u32[]{:S(2)}, u32[]{:S(2)}) async-start(f32[64,1,12]{2,1,0:T(1,128)} %bitcast.7), calls=%async_computation.2 | async-start | bytes 65536 | tf_op jit(solution)/shard_map/all_to_all | solution.py:131
  626.7 10.9 %all-to-all-done.2 = f32[64,1,12]{2,1,0:T(1,128)S(1)} async-done(((f32[64,1,12]{2,1,0:T(1,128)}), f32[64,1,12]{2,1,0:T(1,128)S(1)}, u32[]{:S(2)}, u32[]{:S(2)}) %all-to-all-start.2) | async-done | bytes 3104 | tf_op jit(solution)/shard_map/all_to_all | solution.py:131
  637.7 0.5 broadcast.124
  638.2 0.7 reduce.13
  638.9 0.1 reshape.75
  639.0 1.9 gather_fusion.1
  (36 shorter events, 0.2 us)
Async XLA Ops:
  6.5 279.8 %all-reduce.2.cloned.1.call-start = ((), (), s32[]{:S(2)}) async-start(), calls=%async_computation.3 | async-start | bytes 8388608 | tf_op jit(solution)/shard_map/psum | solution.py:72
  11.8 342.8 %all-gather.5.cloned.1.call-start = ((), (), s32[]{:S(2)}) async-start(), calls=%async_computation.4 | async-start | bytes 5242880 | tf_op jit(solution)/shard_map/all_gather | solution.py:89
  294.8 7.7 %copy-start.3 = (f32[1024,1024]{1,0:T(8,128)}, f32[1024,1024]{1,0:T(8,128)S(1)}, u32[]{:S(2)}) copy-start(f32[1024,1024]{1,0:T(8,128)S(1)} %get-tuple-element.8) | copy-start | bytes 12582916
  307.3 112.4 %all-gather.7.cloned.1.call-start = ((), (), s32[]{:S(2)}) async-start(), calls=%async_computation.5 | async-start | bytes 5242880 | tf_op jit(solution)/shard_map/all_gather | solution.py:89
  354.6 6.3 copy-start
  361.0 3.7 copy-start.5
  369.6 115.4 %all-gather.9.cloned.1.call-start = ((), (), s32[]{:S(2)}) async-start(), calls=%async_computation.6 | async-start | bytes 5242880 | tf_op jit(solution)/shard_map/all_gather | solution.py:89
  419.7 6.6 %copy-start.1 = (f32[1024,1024]{1,0:T(8,128)S(1)}, f32[1024,1024]{1,0:T(8,128)}, u32[]{:S(2)}) copy-start(f32[1024,1024]{1,0:T(8,128)} %all-gather.7.cloned.1.call-done) | copy-start | bytes 12582916
  426.3 3.7 copy-start.4
  434.9 98.2 %all-gather.11.cloned.1.call-start = ((), (), s32[]{:S(2)}) async-start(), calls=%async_computation.7 | async-start | bytes 2621440 | tf_op jit(solution)/shard_map/all_gather | solution.py:91
  485.0 6.3 copy-start.2
  491.3 3.8 copy-start.6
  495.1 4.6 copy-start.8
  495.1 5.5 copy-start.9
  495.1 5.8 copy-start.7
  503.0 38.8 %all-to-all-start = ((bf16[64,1,24]{2,1,0:T(2,128)(2,1)}), bf16[64,1,24]{2,1,0:T(2,128)(2,1)S(1)}, u32[]{:S(2)}, u32[]{:S(2)}) async-start(bf16[64,1,24]{2,1,0:T(2,128)(2,1)} %all_to_all.20), calls=%async_computation | async-start | bytes 65536 | tf_op jit(solution)/shard_map/all_to_all | solution.py:120
  541.8 63.9 %all-to-all-start.1 = ((bf16[64,12,1024]{2,1,0:T(8,128)(2,1)}), bf16[64,12,1024]{2,1,0:T(8,128)(2,1)S(1)}, u32[]{:S(2)}, u32[]{:S(2)}) async-start(bf16[64,12,1024]{2,1,0:T(8,128)(2,1)} %reshape.72), calls=%async_computation.1 | async-start | bytes 4194304 | tf_op jit(solution)/shard_map/all_to_all | solution.py:119
  618.3 19.3 %all-to-all-start.2 = ((f32[64,1,12]{2,1,0:T(1,128)}), f32[64,1,12]{2,1,0:T(1,128)S(1)}, u32[]{:S(2)}, u32[]{:S(2)}) async-start(f32[64,1,12]{2,1,0:T(1,128)} %bitcast.7), calls=%async_computation.2 | async-start | bytes 65536 | tf_op jit(solution)/shard_map/all_to_all | solution.py:131
Sparse Core Ops, SparseCore 0:
  12.8 273.4 all-reduce.1
  307.4 47.1 all-gather.4
  369.7 49.9 all-gather.6
  435.0 49.9 all-gather.8
  499.8 33.2 all-gather.10
where the time goes:
time: 652 us; the launch traced here: 648 us
  waiting for transfers between devices  418 us (64%)
  blocking collectives  78.8 us (12%)
  matrix products  65.2 us (10%)
  starting transfers between devices  34.2 us (5%)
  local copies, waits for them, and re-layouts  23.4 us (4%)
  between operations  14.5 us (2%)
  other arithmetic  13.4 us (2%)
    psum x1, waiting for transfers between devices, local(): lax.psum((lax.dot_general(values, values, (((0,), (0,)), ((), ())), prefe...  196 us
    all_gather x3, waiting for transfers between devices, local(): lax.all_gather(slab_rows, 'rep', axis=0, tiled=True)  147 us
    psum x1, blocking collectives, local(): lax.psum((lax.dot_general(values, values, (((0,), (0,)), ((), ())), prefe...  78.8 us
    all_to_all x1, waiting for transfers between devices, local(): lax.all_to_all(outgoing, 'grp', split_axis=0, concat_axis=0, tiled=True)  46.9 us
    dot_general x8, matrix products, newton_rows(): product = jnp.dot(product, whole, precision=EXACT_MODE)  34 us
    dot_general x4, matrix products, newton_rows(): product = jnp.dot(normed_rows, whole, precision=EXACT_MODE)  23 us
    all_gather x1, waiting for transfers between devices, local(): lax.all_gather(final_rows.astype(jnp.bfloat16), 'rep', axis=0, tiled=True)  17.1 us
  transfers between devices with their start and end apart: 8, of which 7 were waited for; matrix products, arithmetic and copies ran while one was open for 2% of the time, Pallas kernels for 0%

commit v1 on v0

--- a/solution.py
+++ b/solution.py
@@ -70,13 +70,16 @@
     row_total = row_count * lax.axis_size("grp") * lax.axis_size("rep")
     column_part = jnp.sum(values, axis=0, dtype=jnp.float32)
     gram_sum, column_total = lax.psum(
-        (
-            lax.dot_general(
-                values, values, (((0,), (0,)), ((), ())), preferred_element_type=jnp.float32
+        lax.psum(
+            (
+                lax.dot_general(
+                    values, values, (((0,), (0,)), ((), ())), preferred_element_type=jnp.float32
+                ),
+                column_part,
             ),
-            column_part,
+            "grp",
         ),
-        ("grp", "rep"),
+        "rep",
     )
     average, normed = covariance(gram_sum, column_total, row_total)
     share_rows = feat_dim // lax.axis_size("rep")

time: 652 us -> 1270 us (1.95)
  waiting for transfers between devices: 418 us -> 934 us
  blocking collectives: 78.8 us -> 185 us
    psum x1, waiting for transfers between devices: 196 us -> 712 us  [local(): lax.psum((lax.dot_general(values, values, (((0,), (0,)), ((), ())), prefe...]
    psum x1, blocking collectives: 78.8 us -> 179 us  [local(): lax.psum((lax.dot_general(values, values, (((0,), (0,)), ((), ())), prefe...]
  transfers between devices with their start and end apart: 8 -> 9, of which waited for: 7 -> 7; matrix products, arithmetic and copies ran while one was open for 2% -> 1% of each run, Pallas kernels for 0% -> 0%
where the time goes in v1:
time: 1270 us
  waiting for transfers between devices  934 us (74%)
  blocking collectives  185 us (15%)
  matrix products  65.2 us (5%)
  starting transfers between devices  34.3 us (3%)
  local copies, waits for them, and re-layouts  23.4 us (2%)
  between operations  14.8 us (1%)
  other arithmetic  13.4 us (1%)
    psum x1, waiting for transfers between devices, local(): lax.psum((lax.dot_general(values, values, (((0,), (0,)), ((), ())), prefe...  712 us
    psum x1, blocking collectives, local(): lax.psum((lax.dot_general(values, values, (((0,), (0,)), ((), ())), prefe...  179 us
    all_gather x3, waiting for transfers between devices, local(): lax.all_gather(slab_rows, 'rep', axis=0, tiled=True)  147 us
    all_to_all x1, waiting for transfers between devices, local(): lax.all_to_all(outgoing, 'grp', split_axis=0, concat_axis=0, tiled=True)  46.9 us
    dot_general x8, matrix products, newton_rows(): product = jnp.dot(product, whole, precision=EXACT_MODE)  34 us
  transfers between devices with their start and end apart: 9, of which 7 were waited for; matrix products, arithmetic and copies ran while one was open for 1% of the time, Pallas kernels for 0%

profile of v1, /device:TPU:2, one launch (start us, length us, event | category | flops | bytes accessed | tf_op | source)
XLA Modules:
  0.0 1270.9 jit_solution(7862351391408557461)
XLA Ops:
  6.5 0.8 copy.14
  7.4 0.3 mul.102
  7.7 1.4 convert_reduce_fusion
  9.1 2.7 fusion.36
  11.8 0.0 all-reduce.5.cloned.1.call-start
  11.9 712.0 %all-reduce.3.cloned.1.call-done = f32[1024,1024]{1,0:T(8,128)} async-done(((f32[1024,1024]{1,0:T(8,128)}), f32[1024,1024]{1,0:T(8,128)}) %all-reduce.3.cloned.1.call-update) | async-done | bytes 4194320 | tf_op jit(solution)/shard_map/psum | solution.py:73
  723.8 0.0 all-reduce.5.cloned.1.call-update
  723.8 0.0 all-gather.5.cloned.1.call-start
  723.9 179.3 %psum.30 = f32[1024]{0:T(1024)S(1)} all-reduce(f32[1024]{0:T(1024)S(1)} %get-tuple-element.9), channel_id=1, replica_groups=mesh['grp'=64,'rep'=4] {'grp'}, use_global_device_ids=true, to_apply=%region_8.9 | all-reduce | flops 1024 | bytes 8192 | tf_op jit(solution)/shard_map/psum | solution.py:73
  903.1 6.0 psum.31
  909.2 4.2 multiply_reduce_fusion
  914.0 3.6 multiply_subtract_fusion
  917.6 3.8 fusion.14
  921.4 3.8 fusion.33
  925.3 4.8 fusion.4
  930.1 0.0 all-gather.5.cloned.1.call-update
  930.1 0.0 all-gather.7.cloned.1.call-start
  930.2 47.3 %all-gather.5.cloned.1.call-done = f32[1024,1024]{1,0:T(8,128)} async-done(((f32[256,1024]{1,0:T(8,128)}), f32[1024,1024]{1,0:T(8,128)}) %all-gather.5.cloned.1.call-update) | async-done | bytes 4194320 | tf_op jit(solution)/shard_map/all_gather | solution.py:92
  977.5 6.3 fusion.12
  983.9 3.7 fusion.37
  987.6 4.8 fusion.3
  992.4 0.0 all-gather.7.cloned.1.call-update
  992.5 0.0 all-gather.9.cloned.1.call-start
  992.5 50.1 %all-gather.7.cloned.1.call-done = f32[1024,1024]{1,0:T(8,128)} async-done(((f32[256,1024]{1,0:T(8,128)}), f32[1024,1024]{1,0:T(8,128)}) %all-gather.7.cloned.1.call-update) | async-done | bytes 4194320 | tf_op jit(solution)/shard_map/all_gather | solution.py:92
  1042.6 6.6 fusion.10
  1049.2 3.7 fusion.38
  1052.9 4.8 fusion.2
  1057.8 0.0 all-gather.9.cloned.1.call-update
  1057.8 0.0 all-gather.11.cloned.1.call-start
  1057.8 50.1 %all-gather.9.cloned.1.call-done = f32[1024,1024]{1,0:T(8,128)} async-done(((f32[256,1024]{1,0:T(8,128)}), f32[1024,1024]{1,0:T(8,128)}) %all-gather.9.cloned.1.call-update) | async-done | bytes 4194320 | tf_op jit(solution)/shard_map/all_gather | solution.py:92
  1107.9 6.3 fusion.8
  1114.2 3.7 fusion.39
  1118.0 4.6 fusion.5
  1122.6 0.6 reduce-window.6
  1123.3 0.2 slice_reduce_fusion
  1123.5 0.1 copy.12
  1123.6 0.1 fusion.25
  1123.8 1.3 scatter_fusion
  1125.1 0.8 all_to_all.20
  1125.9 13.0 %all-to-all-start = ((bf16[64,1,24]{2,1,0:T(2,128)(2,1)}), bf16[64,1,24]{2,1,0:T(2,128)(2,1)S(1)}, u32[]{:S(2)}, u32[]{:S(2)}) async-start(bf16[64,1,24]{2,1,0:T(2,128)(2,1)} %all_to_all.20), calls=%async_computation | async-start | bytes 65536 | tf_op jit(solution)/shard_map/all_to_all | solution.py:123
  1138.9 17.1 %all-gather.11.cloned.1.call-done = bf16[1024,1024]{1,0:T(8,128)(2,1)} async-done(((bf16[256,1024]{1,0:T(8,128)(2,1)}), bf16[1024,1024]{1,0:T(8,128)(2,1)}) %all-gather.11.cloned.1.call-update) | async-done | bytes 2097168 | tf_op jit(solution)/shard_map/all_gather | solution.py:94
  1156.0 2.5 fusion.40
  1158.5 2.4 multiply_reduce_fusion.1
  1160.9 2.2 scatter_custom_fusion.2
  1163.1 1.5 reshape.72
  1164.7 12.7 all-to-all-start.1
  1177.4 0.1 convert_reduce_fusion.1
  1177.5 0.2 reshape.76
  1177.7 0.4 fusion.22
  1178.1 3.4 scatter_custom_fusion.1
  1181.5 0.1 and.34
  1181.6 46.9 %all-to-all-done.1 = bf16[64,12,1024]{2,1,0:T(8,128)(2,1)S(1)} async-done(((bf16[64,12,1024]{2,1,0:T(8,128)(2,1)}), bf16[64,12,1024]{2,1,0:T(8,128)(2,1)S(1)}, u32[]{:S(2)}, u32[]{:S(2)}) %all-to-all-start.1) | async-done | bytes 1572896 | tf_op jit(solution)/shard_map/all_to_all | solution.py:122
  1228.5 1.3 reshape.121
  1229.8 6.8 scatter_custom_fusion.3
  1236.7 0.6 fusion.6
  1237.3 0.1 max.12
  1237.3 3.2 gather_fusion
  1240.5 0.7 all_to_all.18
  1241.2 8.4 all-to-all-start.2
  1249.6 10.9 all-to-all-done.2
  1260.5 0.5 broadcast.124
  1261.1 0.7 reduce.13
  1261.8 0.1 reshape.75
  1261.9 1.9 gather_fusion.1
  (40 shorter events, 0.3 us)
Async XLA Ops:
  6.5 717.3 %all-reduce.3.cloned.1.call-start = ((), (), s32[]{:S(2)}) async-start(), calls=%async_computation.3 | async-start | bytes 8388608 | tf_op jit(solution)/shard_map/psum | solution.py:73
  11.8 897.3 %all-reduce.5.cloned.1.call-start = ((), (), s32[]{:S(2)}) async-start(), calls=%async_computation.4 | async-start | bytes 8388608 | tf_op jit(solution)/shard_map/psum | solution.py:72
  723.8 253.7 %all-gather.5.cloned.1.call-start = ((), (), s32[]{:S(2)}) async-start(), calls=%async_computation.5 | async-start | bytes 5242880 | tf_op jit(solution)/shard_map/all_gather | solution.py:92
  917.6 7.7 copy-start.3
  930.1 112.5 %all-gather.7.cloned.1.call-start = ((), (), s32[]{:S(2)}) async-start(), calls=%async_computation.6 | async-start | bytes 5242880 | tf_op jit(solution)/shard_map/all_gather | solution.py:92
  977.5 6.3 copy-start
  983.9 3.7 copy-start.5
  992.5 115.4 %all-gather.9.cloned.1.call-start = ((), (), s32[]{:S(2)}) async-start(), calls=%async_computation.7 | async-start | bytes 5242880 | tf_op jit(solution)/shard_map/all_gather | solution.py:92
  1042.6 6.6 copy-start.1
  1049.2 3.7 copy-start.4
  1057.8 98.2 %all-gather.11.cloned.1.call-start = ((), (), s32[]{:S(2)}) async-start(), calls=%async_computation.8 | async-start | bytes 2621440 | tf_op jit(solution)/shard_map/all_gather | solution.py:94
  1107.9 6.3 copy-start.2
  1114.2 3.8 copy-start.6
  1118.0 4.6 copy-start.8
  1118.0 5.5 copy-start.9
  1118.0 5.8 copy-start.7
  1125.9 38.8 %all-to-all-start = ((bf16[64,1,24]{2,1,0:T(2,128)(2,1)}), bf16[64,1,24]{2,1,0:T(2,128)(2,1)S(1)}, u32[]{:S(2)}, u32[]{:S(2)}) async-start(bf16[64,1,24]{2,1,0:T(2,128)(2,1)} %all_to_all.20), calls=%async_computation | async-start | bytes 65536 | tf_op jit(solution)/shard_map/all_to_all | solution.py:123
  1164.7 63.9 %all-to-all-start.1 = ((bf16[64,12,1024]{2,1,0:T(8,128)(2,1)}), bf16[64,12,1024]{2,1,0:T(8,128)(2,1)S(1)}, u32[]{:S(2)}, u32[]{:S(2)}) async-start(bf16[64,12,1024]{2,1,0:T(8,128)(2,1)} %reshape.72), calls=%async_computation.1 | async-start | bytes 4194304 | tf_op jit(solution)/shard_map/all_to_all | solution.py:122
  1241.2 19.3 %all-to-all-start.2 = ((f32[64,1,12]{2,1,0:T(1,128)}), f32[64,1,12]{2,1,0:T(1,128)S(1)}, u32[]{:S(2)}, u32[]{:S(2)}) async-start(f32[64,1,12]{2,1,0:T(1,128)} %bitcast.7), calls=%async_computation.2 | async-start | bytes 65536 | tf_op jit(solution)/shard_map/all_to_all | solution.py:134
Sparse Core Ops, SparseCore 0:
  11.9 711.8 all-reduce.2
  726.5 95.2 all-reduce.4
  930.3 47.2 all-gather.4
  992.6 49.9 all-gather.6
  1057.9 49.9 all-gather.8
  1122.7 33.2 all-gather.10
